TPU v7x, 32 devices: a whole 2x2x4 slice. The times are simulated.
32 devices in a mesh: box: 8 (over z, y), nbr: 4 (over x, core).
Axes of the slice: x: 2, y: 2, z: 4, core: 2. Of those that a mesh axis runs over, the one named last changes fastest.
Arguments:
- self_block: float32 [64, 256, 256], P('box', 'nbr'), as said below
- ordering: int32 [64, 256], P('box'), may hold values from 0 to 255, each once within a row
- interp: float32 [64, 64, 192], P('box'), may hold values from -0.12 to 0.12
- near_band: float32 [64, 8, 2, 64, 256], P('box', 'nbr'), may hold values from -3 to 3
- pair_mask: int32 [64, 8], P('box', 'nbr'), may hold values 0 or 1
Outputs:
- skeleton_self: float32 [64, 64, 64], P('box')
- red_inverse: float32 [64, 192, 192], P('box', 'nbr')
- couplings: float32 [64, 8, 64, 128], P('box', 'nbr')
Inputs may be any that keep to these rules, and one draw needn't show every extreme that they name: Each row of ordering is a permutation of the 256 unknowns of its box. Each self_block[b] has a positive diagonal.
All inputs are finite; a program needn't handle non-finite values. No bound on the sum of `pair_mask` on one device may be relied on, other than what follows from the above.
Results may differ from a plain program's by a relative error of at most 0.0003.
Values sent between devices are 32-bit elements; how exact they have to be, the bound alone decides.
A program may use at most 128 MiB of HBM per device.

v0:
```python
import jax
import jax.numpy as jnp
from jax import lax
from jax.sharding import PartitionSpec as P

SKEL = 64
RED = 192
REACH = 4
NS_ITERS = 3


def extended_2(block, sides, width):
    for axis, dim in sides:
        count = lax.axis_size(axis)
        forward = [(i, i + 1) for i in range(count - 1)]
        forward.append((count - 1, 0))
        backward = [(target, source) for source, target in forward]
        low = lax.ppermute(
            lax.slice_in_dim(block, block.shape[dim] - width, None, axis=dim), axis, forward
        )
        high = lax.ppermute(lax.slice_in_dim(block, 0, width, axis=dim), axis, backward)
        block = jnp.concatenate([low, block, high], axis=dim)
    return block


def passed_along(block, axis, distance):
    devices = range(lax.axis_size(axis))
    route = [((i - distance) % len(devices), i) for i in devices]
    return lax.ppermute(block, axis, route)


def product(pattern, left_term, right_term):
    return jnp.einsum(pattern, left_term, right_term, precision=lax.Precision.HIGHEST)


def selector(ordering):
    columns = jnp.arange(ordering.shape[1], dtype=jnp.int32)
    return (ordering[:, :, None] == columns[None, None, :]).astype(jnp.float32)


def permuted(matrix, chooser):
    row_sorted = product("bik,bkj->bij", chooser, matrix)
    return product("bik,bjk->bij", row_sorted, chooser)


def factors(matrix, chooser, interp):
    full_block = permuted(matrix, chooser)
    skel_skel = full_block[:, :SKEL, :SKEL]
    skel_red = full_block[:, :SKEL, SKEL:]
    red_skel = full_block[:, SKEL:, :SKEL]
    red_red = full_block[:, SKEL:, SKEL:]
    skel_interp = product("bij,bjk->bik", skel_skel, interp)
    x_skel_red = skel_red - skel_interp
    x_red_skel = red_skel - product("bji,bjk->bik", interp, skel_skel)
    x_red_red = (
        red_red
        - product("bji,bjk->bik", interp, skel_red)
        - product("bij,bjk->bik", red_skel, interp)
    )
    x_red_red = x_red_red + product("bji,bjk->bik", interp, skel_interp)
    identity = jnp.eye(RED, dtype=jnp.float32)
    diag_vals = jnp.diagonal(red_red, axis1=1, axis2=2)
    approx = identity[None] / diag_vals[:, None, :]
    for sweep_index in range(NS_ITERS):
        approx = 2.0 * approx - product(
            "bij,bjk->bik", approx, product("bij,bjk->bik", x_red_red, approx)
        )
    left_factor = product("bij,bjk->bik", x_skel_red, approx)
    right_factor = product("bij,bjk->bik", approx, x_red_skel)
    own_block = skel_skel - product("bij,bjk->bik", left_factor, x_red_skel)
    return (approx, left_factor, right_factor, own_block)


def slot_terms(near_piece, chooser, interp, approx, left_factor, right_factor):
    both_parts = product("bpik,bjk->bpij", near_piece, chooser)
    row_part = both_parts[:, 0]
    col_part = both_parts[:, 1]
    near_red = row_part[:, :, SKEL:] - product("bij,bjk->bik", row_part[:, :, :SKEL], interp)
    red_near_t = col_part[:, :, SKEL:] - product("bij,bjk->bik", col_part[:, :, :SKEL], interp)
    new_forward = jnp.swapaxes(col_part[:, :, :SKEL], 1, 2) - product(
        "bij,bkj->bik", left_factor, red_near_t
    )
    new_backward = jnp.swapaxes(row_part[:, :, :SKEL], 1, 2) - product(
        "bji,bkj->bik", right_factor, near_red
    )
    coupled = jnp.concatenate([new_forward, new_backward], axis=2)
    update = product("bij,bkj->bik", product("bij,bjk->bik", near_red, approx), red_near_t)
    return (coupled, update)


def body(self_block, ordering, interp, near_band, pair_mask):
    box_count = ordering.shape[0]
    nbr_count = lax.axis_size("nbr")
    nbr_place = lax.axis_index("nbr")
    chooser = selector(ordering)
    share_boxes = box_count // nbr_count
    own_rows = lax.all_to_all(self_block, "nbr", split_axis=0, concat_axis=1, tiled=True)
    my_chooser = lax.dynamic_slice_in_dim(chooser, nbr_place * share_boxes, share_boxes, 0)
    my_interp = lax.dynamic_slice_in_dim(interp, nbr_place * share_boxes, share_boxes, 0)
    part_inverse, part_left, part_right, part_own = factors(own_rows, my_chooser, my_interp)
    approx, left_factor, right_factor, own_block = (
        lax.all_gather(part_inverse, "nbr", axis=0, tiled=True),
        lax.all_gather(part_left, "nbr", axis=0, tiled=True),
        lax.all_gather(part_right, "nbr", axis=0, tiled=True),
        lax.all_gather(part_own, "nbr", axis=0, tiled=True),
    )
    masked = near_band * pair_mask.astype(jnp.float32)[:, :, None, None, None]
    local_slots = near_band.shape[1]
    windows = []
    widened = extended_2(masked, (("box", 0),), REACH)
    for slot_index in range(local_slots):
        windows.append((widened[:, slot_index], REACH))
    extended = jnp.zeros((box_count + 2 * REACH, SKEL, SKEL), jnp.float32)
    couples = []
    for slot_index in range(local_slots):
        window, margin = windows[slot_index]
        global_slot = nbr_place * local_slots + slot_index
        offset = jnp.where(global_slot < REACH, global_slot - REACH, global_slot - REACH + 1)
        near_piece = lax.dynamic_slice_in_dim(window, margin - offset, box_count, 0)
        coupled, update = slot_terms(near_piece, chooser, interp, approx, left_factor, right_factor)
        couples.append(coupled)
        extended = extended + lax.dynamic_update_slice_in_dim(
            jnp.zeros_like(extended), update, REACH - offset, 0
        )
    incoming_right = passed_along(extended[:REACH], "box", -1)
    incoming_left = passed_along(extended[REACH + box_count :], "box", 1)
    owned_sum = extended[REACH : REACH + box_count]
    owned_sum = owned_sum.at[box_count - REACH :].add(incoming_right)
    owned_sum = owned_sum.at[:REACH].add(incoming_left)
    update_total = lax.psum(owned_sum, "nbr")
    skeleton_self = own_block - update_total
    row_count = approx.shape[1] // nbr_count
    red_inverse = lax.dynamic_slice_in_dim(approx, nbr_place * row_count, row_count, 1)
    return (skeleton_self, red_inverse, jnp.stack(couples, 1))


def solution(mesh):
    placed = (
        P("box", "nbr", None),
        P("box", None),
        P("box", None, None),
        P("box", "nbr", None, None, None),
        P("box", "nbr"),
    )
    return jax.shard_map(
        body,
        mesh=mesh,
        in_specs=placed,
        out_specs=(P("box", None, None), P("box", "nbr", None), P("box", "nbr", None, None)),
        check_vma=False,
    )
```

profile of v0, /device:TPU:0, one launch (start us, length us, event | category | flops | bytes accessed | tf_op | source)
XLA Modules:
  0.0 154.4 jit_solution(4811347467437603980)
XLA Ops:
  7.2 4.4 %all-to-all-start = ((f32[8,64,256]{2,1,0:T(8,128)}), f32[8,64,256]{2,1,0:T(8,128)S(1)}, u32[]{:S(2)}, u32[]{:S(2)}) async-start(f32[8,64,256]{2,1,0:T(8,128)} %param.9), calls=%async_computation | async-start | bytes 1048576 | tf_op jit(solution)/shard_map/all_to_all | solution.py:97
  11.6 0.7 convert_element_type.12
  12.2 0.1 copy.79
  12.3 1.9 %broadcast_multiply_fusion = f32[8,2,2,64,256]{4,3,2,1,0:T(8,128)S(1)} fusion(f32[8,2,2,64,256]{4,3,2,1,0:T(8,128)} %param.12, f32[8,2]{1,0:T(8,128)S(1)} %copy.79), kind=kLoop, calls=%fused_computation.31 | loop fusion | flops 524288 | bytes 4194368 | tf_op jit(solution)/shard_map/mul | solution.py:107
  14.2 1.5 fusion.50
  15.8 2.3 %collective-permute-start = (f32[4,2,2,64,256]{4,3,2,1,0:T(8,128)}, f32[4,2,2,64,256]{4,3,2,1,0:T(8,128)}, u32[]{:S(2)}, u32[]{:S(2)}) collective-permute-start(f32[4,2,2,64,256]{4,3,2,1,0:T(8,128)} %get-tuple-element.44), channel_id=1, source_target_pairs={{0,4},{4,8},{8,12},{12,16},{16,20},{20,24},{24,28},{28,0},{1,5},{5... | collective-permute-start | bytes 3145736 | tf_op jit(solution)/shard_map/ppermute | solution.py:18
  18.1 3.0 %collective-permute-start.1 = (f32[4,2,2,64,256]{4,3,2,1,0:T(8,128)}, f32[4,2,2,64,256]{4,3,2,1,0:T(8,128)}, u32[]{:S(2)}, u32[]{:S(2)}) collective-permute-start(f32[4,2,2,64,256]{4,3,2,1,0:T(8,128)} %get-tuple-element.45), channel_id=1, source_target_pairs={{4,0},{8,4},{12,8},{16,12},{20,16},{24,20},{28,24},{0,28},{5,1},{9... | collective-permute-start | bytes 3145736 | tf_op jit(solution)/shard_map/ppermute | solution.py:21
  21.1 0.7 fusion.25
  21.8 1.1 iota_compare_fusion
  23.0 1.4 fusion.12
  24.3 1.3 fusion.10
  25.7 0.6 convolution_subtract_fusion.5
  26.3 0.9 fusion.36
  27.2 0.9 slice.151
  28.1 0.7 slice.152
  28.8 0.5 convolution_subtract_fusion.4
  29.3 10.5 %copy.75 = f32[2,192,192]{0,2,1:T(8,128)} copy(f32[2,192,192]{2,1,0:T(8,128)} %slice.151) | data formatting | bytes 589824 | tf_op jit(solution)/shard_map/slice | solution.py:51
  39.8 5.2 %gather_fusion = f32[192,2]{1,0:T(8,128)} fusion(f32[2,192,192]{0,2,1:T(8,128)} %copy.75, s32[192]{0:T(256)S(1)} %bitcast.80), kind=kCustom, calls=%fused_computation | custom fusion | bytes 4608 | tf_op jit(solution)/shard_map/jit(diagonal)/gather | solution.py:62
  45.0 1.0 copy.76
  46.0 1.5 convolution_add_fusion
  47.5 1.5 fusion.14
  49.0 0.6 convolution_subtract_fusion.8
  49.5 0.5 fusion.52
  50.1 0.5 convolution_subtract_fusion.7
  50.6 0.5 fusion.53
  51.2 0.5 convolution_subtract_fusion.6
  51.7 2.1 %fusion.28 = f32[2,64,192]{2,1,0:T(8,128)} fusion(f32[2,192,192]{2,1,0:T(8,128)S(1)} %convolution_subtract_fusion.6, f32[2,64,192]{2,1,0:T(8,128)} %fusion.36, f32[2,256,256]{2,1,0:T(8,128)S(1)} %fusion.10), kind=kOutput, calls=%fused_computation.61 | convolution fusion | flops 56647680 | bytes 720896 | tf_op jit(solution)/shard_map/bij,bjk->bik/dot_general | solution.py:33
  53.8 0.0 all-reduce.2.cloned.1.call-start
  53.9 1.8 %copy.96 = f32[2,192,64]{1,2,0:T(8,128)} copy(f32[2,192,64]{2,1,0:T(8,128)} %slice.152) | data formatting | bytes 196608
  55.6 1.2 convolution_subtract_fusion.13
  56.9 1.2 convolution_subtract_fusion.14
  58.0 7.4 %all_gather.12 = f32[8,64,64]{2,1,0:T(8,128)} all-gather(f32[2,64,64]{2,1,0:T(8,128)S(1)} %convolution_subtract_fusion.14), channel_id=1, replica_groups=mesh['box'=8,'nbr'=4] {'nbr'}, dimensions={0}, use_global_device_ids=true | all-gather | bytes 163840 | tf_op jit(solution)/shard_map/all_gather | solution.py:105
  65.4 10.1 %all_gather.14 = f32[8,64,192]{2,1,0:T(8,128)S(1)} all-gather(f32[2,64,192]{2,1,0:T(8,128)} %fusion.28), channel_id=1, replica_groups=mesh['box'=8,'nbr'=4] {'nbr'}, dimensions={0}, use_global_device_ids=true | all-gather | bytes 491520 | tf_op jit(solution)/shard_map/all_gather | solution.py:103
  75.5 0.5 fusion.56
  76.0 7.5 %all_gather.15 = f32[8,192,64]{1,2,0:T(8,128)S(1)} all-gather(f32[2,192,64]{1,2,0:T(8,128)S(1)} %fusion.56), channel_id=1, replica_groups=mesh['box'=8,'nbr'=4] {'nbr'}, dimensions={0}, use_global_device_ids=true | all-gather | bytes 491520 | tf_op jit(solution)/shard_map/all_gather | solution.py:104
  83.5 2.0 %pad_maximum_fusion = f32[16,2,2,64,256]{4,3,2,1,0:T(8,128)S(1)} fusion(f32[4,2,2,64,256]{4,3,2,1,0:T(8,128)} %collective-permute-done.1, f32[8,2,2,64,256]{4,3,2,1,0:T(8,128)S(1)} %broadcast_multiply_fusion, f32[4,2,2,64,256]{4,3,2,1,0:T(8,128)} %collective-permute-done), kind=kLoop, calls=%fused_computation.1 | loop fusion | flops 2097152 | bytes 8388608 | tf_op jit(solution)/shard_map/concatenate | solution.py:22
  85.5 0.4 fusion.49
  85.9 1.6 %fusion.2 = f32[8,2,64,256]{3,2,0,1:T(8,128)S(1)} fusion(s32[8,256]{1,0:T(8,128)S(1)} %copy-done.14, f32[16,1,2,64,256]{4,3,2,1,0:T(8,128)S(1)} %get-tuple-element.42, s32[]{:T(128)S(6)} %select_n.30), kind=kOutput, calls=%fused_computation.5 | convolution fusion | flops 805830656 | bytes 2105348 | tf_op jit(solution)/shard_map/bpik,bjk->bpij/dot_general | solution.py:33
  87.5 0.1 slice_bitcast_fusion
  87.6 0.6 convolution_subtract_fusion
  88.2 1.6 %fusion = f32[8,2,64,256]{3,2,1,0:T(8,128)S(1)} fusion(f32[16,1,2,64,256]{4,3,2,1,0:T(8,128)S(1)} %get-tuple-element.43, s32[]{:T(128)S(6)} %select_n.28, s32[8,256]{1,0:T(8,128)S(1)} %copy-done.14), kind=kOutput, calls=%fused_computation.3 | convolution fusion | flops 805830656 | bytes 2105348 | tf_op jit(solution)/shard_map/bpik,bjk->bpij/dot_general | solution.py:33
  89.8 0.1 slice_bitcast_fusion.2
  89.9 0.6 convolution_subtract_fusion.1
  90.5 0.6 convolution_subtract_fusion.2
  91.1 0.6 convolution_subtract_fusion.3
  91.7 0.7 convolution_subtract_fusion.10
  92.4 0.7 convolution_subtract_fusion.12
  93.0 0.7 convolution_subtract_fusion.9
  93.7 0.7 convolution_subtract_fusion.11
  94.4 1.1 maximum_bitcast_fusion
  95.5 2.8 %fusion.54 = f32[8,64,192]{2,1,0:T(8,128)S(1)} fusion(f32[8,64,192]{2,1,0:T(8,128)} %copy-done.4, f32[8,192,192]{2,1,0:T(8,128)} %all-gather.2.cloned.1.call-done), kind=kOutput, calls=%fused_computation.89 | convolution fusion | flops 226492416 | bytes 1966080 | tf_op jit(solution)/shard_map/bij,bjk->bik/dot_general | solution.py:33
  98.3 0.6 convolution_dynamic-update-slice_fusion
  99.0 1.1 fusion.55
  100.2 0.6 fusion.4
  100.8 0.8 copy-done.7
  101.7 2.3 %collective-permute-start.2 = (f32[4,64,64]{2,1,0:T(8,128)S(1)}, f32[4,64,64]{2,1,0:T(8,128)S(1)}, u32[]{:S(2)}, u32[]{:S(2)}) collective-permute-start(f32[4,64,64]{2,1,0:T(8,128)S(1)} %get-tuple-element.51), channel_id=1, source_target_pairs={{4,0},{8,4},{12,8},{16,12},{20,16},{24,20},{28,24},{0,28},{5,1},{9... | collective-permute-start | bytes 196616 | tf_op jit(solution)/shard_map/ppermute | solution.py:29
  103.9 1.1 pad_maximum_fusion.1
  105.0 2.4 %copy.87 = f32[8,2,64,128]{3,2,1,0:T(8,128)} copy(f32[8,2,64,128]{2,3,0,1:T(8,128)} %pad_maximum_fusion.1) | data formatting | bytes 1048576
  107.4 0.1 collective-permute-start.3
  107.5 8.1 %collective-permute-done.3 = f32[4,64,64]{2,1,0:T(8,128)S(1)} collective-permute-done((f32[4,64,64]{2,1,0:T(8,128)S(1)}, f32[4,64,64]{2,1,0:T(8,128)S(1)}, u32[]{:S(2)}, u32[]{:S(2)}) %collective-permute-start.3) | collective-permute-done | bytes 65568 | tf_op jit(solution)/shard_map/ppermute | solution.py:29
  115.7 0.7 copy-done.11
  116.4 0.8 constant_dynamic-slice_fusion
  117.2 28.7 %all-reduce.2.cloned.1.call-done = f32[8,64,64]{2,1,0:T(8,128)} async-done(((f32[8,64,64]{2,1,0:T(8,128)}), f32[8,64,64]{2,1,0:T(8,128)}) %all-reduce.2.cloned.1.call-update) | async-done | bytes 131088 | tf_op jit(solution)/shard_map/psum | solution.py:130
  145.9 1.7 %sub.80 = f32[8,64,64]{2,1,0:T(8,128)} subtract(f32[8,64,64]{2,1,0:T(8,128)S(1)} %copy-done.12, f32[8,64,64]{2,1,0:T(8,128)} %all-reduce.2.cloned.1.call-done) | non-fusion elementwise | flops 32768 | bytes 393216 | tf_op jit(solution)/shard_map/sub | solution.py:131
  (43 shorter events, 0.3 us)
Async XLA Ops:
  7.2 18.5 %copy-start = (f32[8,64,192]{2,1,0:T(8,128)S(1)}, f32[8,64,192]{2,1,0:T(8,128)}, u32[]{:S(2)}) copy-start(f32[8,64,192]{2,1,0:T(8,128)} %param.11) | copy-start | bytes 1179652
  7.2 15.8 %all-to-all-start = ((f32[8,64,256]{2,1,0:T(8,128)}), f32[8,64,256]{2,1,0:T(8,128)S(1)}, u32[]{:S(2)}, u32[]{:S(2)}) async-start(f32[8,64,256]{2,1,0:T(8,128)} %param.9), calls=%async_computation | async-start | bytes 1048576 | tf_op jit(solution)/shard_map/all_to_all | solution.py:97
  11.6 83.9 %all-gather.2.cloned.1.call-start = ((), (), s32[]{:S(2)}) async-start(), calls=%async_computation.1 | async-start | bytes 1966080 | tf_op jit(solution)/shard_map/all_gather | solution.py:102
  14.2 7.6 %copy-start.14 = (s32[8,256]{1,0:T(8,128)S(1)}, s32[8,256]{1,0:T(8,128)}, u32[]{:S(2)}) copy-start(s32[8,256]{1,0:T(8,128)} %param.10) | copy-start | bytes 24580
  15.8 67.7 %collective-permute-start = (f32[4,2,2,64,256]{4,3,2,1,0:T(8,128)}, f32[4,2,2,64,256]{4,3,2,1,0:T(8,128)}, u32[]{:S(2)}, u32[]{:S(2)}) collective-permute-start(f32[4,2,2,64,256]{4,3,2,1,0:T(8,128)} %get-tuple-element.44), channel_id=1, source_target_pairs={{0,4},{4,8},{8,12},{12,16},{16,20},{20,24},{24,28},{28,0},{1,5},{5... | collective-permute-start | bytes 3145736 | tf_op jit(solution)/shard_map/ppermute | solution.py:18
  18.1 65.4 %collective-permute-start.1 = (f32[4,2,2,64,256]{4,3,2,1,0:T(8,128)}, f32[4,2,2,64,256]{4,3,2,1,0:T(8,128)}, u32[]{:S(2)}, u32[]{:S(2)}) collective-permute-start(f32[4,2,2,64,256]{4,3,2,1,0:T(8,128)} %get-tuple-element.45), channel_id=1, source_target_pairs={{4,0},{8,4},{12,8},{16,12},{20,16},{24,20},{28,24},{0,28},{5,1},{9... | collective-permute-start | bytes 3145736 | tf_op jit(solution)/shard_map/ppermute | solution.py:21
  46.0 3.0 %copy-start.13 = (f32[192,192]{1,0:T(8,128)S(1)}, f32[192,192]{1,0:T(8,128)}, u32[]{:S(2)}) copy-start(f32[192,192]{1,0:T(8,128)} %fusion.25) | copy-start | bytes 442372
  51.7 2.1 %copy-start.2 = (f32[2,192,192]{2,1,0:T(8,128)}, f32[2,192,192]{2,1,0:T(8,128)S(1)}, u32[]{:S(2)}) copy-start(f32[2,192,192]{2,1,0:T(8,128)S(1)} %convolution_subtract_fusion.6) | copy-start | bytes 884740
  53.8 21.7 %copy-start.3 = (f32[2,192,192]{2,1,0:T(8,128)S(1)}, f32[2,192,192]{2,1,0:T(8,128)}, u32[]{:S(2)}) copy-start(f32[2,192,192]{2,1,0:T(8,128)} %copy-done.2) | copy-start | bytes 884740
  53.8 92.0 %all-reduce.2.cloned.1.call-start = ((), (), s32[]{:S(2)}) async-start(), calls=%async_computation.2 | async-start | bytes 524288 | tf_op jit(solution)/shard_map/psum | solution.py:130
  88.2 3.5 %copy-start.5 = (f32[8,64,192]{2,1,0:T(8,128)}, f32[8,64,192]{2,1,0:T(8,128)S(1)}, u32[]{:S(2)}) copy-start(f32[8,64,192]{2,1,0:T(8,128)S(1)} %convolution_subtract_fusion) | copy-start | bytes 1179652
  91.7 2.0 %copy-start.4 = (f32[8,64,192]{2,1,0:T(8,128)}, f32[8,64,192]{2,1,0:T(8,128)S(1)}, u32[]{:S(2)}) copy-start(f32[8,64,192]{2,1,0:T(8,128)S(1)} %convolution_subtract_fusion.3) | copy-start | bytes 1179652
  95.5 3.5 %copy-start.1 = (f32[8,192,192]{2,1,0:T(8,128)S(1)}, f32[8,192,192]{2,1,0:T(8,128)}, u32[]{:S(2)}) copy-start(f32[8,192,192]{2,1,0:T(8,128)} %all-gather.2.cloned.1.call-done) | copy-start | bytes 3538948
  98.3 1.8 %copy-start.6 = (f32[8,64,192]{2,1,0:T(8,128)S(1)}, f32[8,64,192]{2,1,0:T(8,128)}, u32[]{:S(2)}) copy-start(f32[8,64,192]{2,1,0:T(8,128)} %copy-done.5) | copy-start | bytes 1179652
  99.0 4.9 %copy-start.9 = (f32[8,1,64,128]{2,3,0,1:T(8,128)S(1)}, f32[8,1,64,128]{2,3,0,1:T(8,128)}, u32[]{:S(2)}) copy-start(f32[8,1,64,128]{2,3,0,1:T(8,128)} %get-tuple-element.52) | copy-start | bytes 786436
  99.0 4.9 %copy-start.10 = (f32[8,1,64,128]{2,3,0,1:T(8,128)S(1)}, f32[8,1,64,128]{2,3,0,1:T(8,128)}, u32[]{:S(2)}) copy-start(f32[8,1,64,128]{2,3,0,1:T(8,128)} %get-tuple-element.53) | copy-start | bytes 786436
  100.8 0.8 copy-start.7
  101.7 5.7 %copy-start.8 = (f32[16,64,64]{2,1,0:T(8,128)S(1)}, f32[16,64,64]{2,1,0:T(8,128)}, u32[]{:S(2)}) copy-start(f32[16,64,64]{2,1,0:T(8,128)} %copy-done.7) | copy-start | bytes 786436
  101.7 5.8 %collective-permute-start.2 = (f32[4,64,64]{2,1,0:T(8,128)S(1)}, f32[4,64,64]{2,1,0:T(8,128)S(1)}, u32[]{:S(2)}, u32[]{:S(2)}) collective-permute-start(f32[4,64,64]{2,1,0:T(8,128)S(1)} %get-tuple-element.51), channel_id=1, source_target_pairs={{4,0},{8,4},{12,8},{16,12},{20,16},{24,20},{28,24},{0,28},{5,1},{9... | collective-permute-start | bytes 196616 | tf_op jit(solution)/shard_map/ppermute | solution.py:29
  105.0 40.9 %copy-start.12 = (f32[8,64,64]{2,1,0:T(8,128)S(1)}, f32[8,64,64]{2,1,0:T(8,128)}, u32[]{:S(2)}) copy-start(f32[8,64,64]{2,1,0:T(8,128)} %all_gather.12) | copy-start | bytes 393220
  107.4 8.2 %collective-permute-start.3 = (f32[4,64,64]{2,1,0:T(8,128)S(1)}, f32[4,64,64]{2,1,0:T(8,128)S(1)}, u32[]{:S(2)}, u32[]{:S(2)}) collective-permute-start(f32[4,64,64]{2,1,0:T(8,128)S(1)} %get-tuple-element.50), channel_id=1, source_target_pairs={{28,0},{0,4},{4,8},{8,12},{12,16},{16,20},{20,24},{24,28},{29,1},{... | collective-permute-start | bytes 196616 | tf_op jit(solution)/shard_map/ppermute | solution.py:29
  115.7 0.7 copy-start.11
Sparse Core Ops, SparseCore 0:
  53.9 20.9 all-gather.1
  116.5 29.3 all-reduce.1
where the time goes:
time: 155 us; the launch traced here: 154 us
  waiting for transfers between devices  36.9 us (24%)
  matrix products  28.6 us (18%)
  local copies, waits for them, and re-layouts  27.1 us (17%)
  blocking collectives  24.9 us (16%)
  between operations  14.5 us (9%)
  starting transfers between devices  12.1 us (8%)
  other arithmetic  10.3 us (7%)
    psum x1, waiting for transfers between devices, body(): update_total = lax.psum(owned_sum, 'nbr')  28.7 us
    dot_general x30, matrix products, product(): jnp.einsum(pattern, left_term, right_term, precision=lax.Precision.HIGHEST)  28.6 us
    slice x2, local copies, waits for them, and re-layouts, factors(): red_red = full_block[:, SKEL:, SKEL:]  11.4 us
    all_gather x1, blocking collectives, body(): lax.all_gather(part_left, 'nbr', axis=0, tiled=True)  10.1 us
    ppermute x2, waiting for transfers between devices, passed_along(): return lax.ppermute(block, axis, route)  8.12 us
    all_gather x1, blocking collectives, body(): lax.all_gather(part_right, 'nbr', axis=0, tiled=True)  7.46 us
    all_gather x1, blocking collectives, body(): lax.all_gather(part_own, 'nbr', axis=0, tiled=True)  7.4 us
    unnamed x33, local copies, waits for them, and re-layouts  6.4 us
  transfers between devices with their start and end apart: 7, of which 2 were waited for; matrix products, arithmetic and copies ran while one was open for 37% of the time, Pallas kernels for 0%

commit v1 on v0

--- a/solution.py
+++ b/solution.py
@@ -127,7 +127,7 @@
     owned_sum = extended[REACH : REACH + box_count]
     owned_sum = owned_sum.at[box_count - REACH :].add(incoming_right)
     owned_sum = owned_sum.at[:REACH].add(incoming_left)
-    update_total = lax.psum(owned_sum, "nbr")
+    update_total = jnp.sum(lax.all_gather(owned_sum, "nbr"), axis=0)
     skeleton_self = own_block - update_total
     row_count = approx.shape[1] // nbr_count
     red_inverse = lax.dynamic_slice_in_dim(approx, nbr_place * row_count, row_count, 1)

time: 155 us -> 131 us (0.85)
  waiting for transfers between devices: 36.9 us -> 7.05 us
  blocking collectives: 24.9 us -> 34.8 us
  other arithmetic: 10.3 us -> 8.48 us
    psum x1 -> x0, waiting for transfers between devices: 28.7 us -> none  [body(): update_total = lax.psum(owned_sum, 'nbr')]
    all_gather x0 -> x1, blocking collectives: none -> 9.85 us  [body(): update_total = jnp.sum(lax.all_gather(owned_sum, 'nbr'), axis=0)]
    unnamed x33 -> x16, local copies, waits for them, and re-layouts: 6.4 us -> 4.83 us
  transfers between devices with their start and end apart: 7 -> 6, of which waited for: 2 -> 2; matrix products, arithmetic and copies ran while one was open for 37% -> 43% of each run, Pallas kernels for 0% -> 0%
where the time goes in v1:
time: 131 us
  blocking collectives  34.8 us (27%)
  matrix products  28.5 us (22%)
  local copies, waits for them, and re-layouts  25.6 us (20%)
  between operations  14.4 us (11%)
  starting transfers between devices  11.8 us (9%)
  other arithmetic  8.48 us (6%)
  waiting for transfers between devices  7.05 us (5%)
    dot_general x30, matrix products, product(): jnp.einsum(pattern, left_term, right_term, precision=lax.Precision.HIGHEST)  28.5 us
    slice x2, local copies, waits for them, and re-layouts, factors(): red_red = full_block[:, SKEL:, SKEL:]  11.4 us
    all_gather x1, blocking collectives, body(): lax.all_gather(part_left, 'nbr', axis=0, tiled=True)  10.5 us
    all_gather x1, blocking collectives, body(): update_total = jnp.sum(lax.all_gather(owned_sum, 'nbr'), axis=0)  9.85 us
    all_gather x1, blocking collectives, body(): lax.all_gather(part_right, 'nbr', axis=0, tiled=True)  7.46 us
    ppermute x2, waiting for transfers between devices, passed_along(): return lax.ppermute(block, axis, route)  7.02 us
    all_gather x1, blocking collectives, body(): lax.all_gather(part_own, 'nbr', axis=0, tiled=True)  6.91 us
    gather x2, local copies, waits for them, and re-layouts, factors(): diag_vals = jnp.diagonal(red_red, axis1=1, axis2=2)  6.29 us
  transfers between devices with their start and end apart: 6, of which 2 were waited for; matrix products, arithmetic and copies ran while one was open for 43% of the time, Pallas kernels for 0%

profile of v1, /device:TPU:0, one launch (start us, length us, event | category | flops | bytes accessed | tf_op | source)
XLA Modules:
  0.0 130.6 jit_solution(10462875051046469908)
XLA Ops:
  7.2 4.4 %all-to-all-start = ((f32[8,64,256]{2,1,0:T(8,128)}), f32[8,64,256]{2,1,0:T(8,128)S(1)}, u32[]{:S(2)}, u32[]{:S(2)}) async-start(f32[8,64,256]{2,1,0:T(8,128)} %param.9), calls=%async_computation | async-start | bytes 1048576 | tf_op jit(solution)/shard_map/all_to_all | solution.py:97
  11.6 0.7 convert_element_type.12
  12.2 0.1 copy.79
  12.3 1.9 %broadcast_multiply_fusion = f32[8,2,2,64,256]{4,3,2,1,0:T(8,128)S(1)} fusion(f32[8,2,2,64,256]{4,3,2,1,0:T(8,128)} %param.12, f32[8,2]{1,0:T(8,128)S(1)} %copy.79), kind=kLoop, calls=%fused_computation.31 | loop fusion | flops 524288 | bytes 4194368 | tf_op jit(solution)/shard_map/mul | solution.py:107
  14.2 1.6 %fusion.51 = (f32[4,2,2,64,256]{4,3,2,1,0:T(8,128)}, f32[4,2,2,64,256]{4,3,2,1,0:T(8,128)}) fusion(f32[8,2,2,64,256]{4,3,2,1,0:T(8,128)S(1)} %broadcast_multiply_fusion), kind=kLoop, calls=%fused_computation.86 | loop fusion | bytes 4194304 | tf_op jit(solution)/shard_map/slice | solution.py:19
  15.8 2.3 %collective-permute-start = (f32[4,2,2,64,256]{4,3,2,1,0:T(8,128)}, f32[4,2,2,64,256]{4,3,2,1,0:T(8,128)}, u32[]{:S(2)}, u32[]{:S(2)}) collective-permute-start(f32[4,2,2,64,256]{4,3,2,1,0:T(8,128)} %get-tuple-element.44), channel_id=1, source_target_pairs={{0,4},{4,8},{8,12},{12,16},{16,20},{20,24},{24,28},{28,0},{1,5},{5... | collective-permute-start | bytes 3145736 | tf_op jit(solution)/shard_map/ppermute | solution.py:18
  18.1 3.0 %collective-permute-start.1 = (f32[4,2,2,64,256]{4,3,2,1,0:T(8,128)}, f32[4,2,2,64,256]{4,3,2,1,0:T(8,128)}, u32[]{:S(2)}, u32[]{:S(2)}) collective-permute-start(f32[4,2,2,64,256]{4,3,2,1,0:T(8,128)} %get-tuple-element.45), channel_id=1, source_target_pairs={{4,0},{8,4},{12,8},{16,12},{20,16},{24,20},{28,24},{0,28},{5,1},{9... | collective-permute-start | bytes 3145736 | tf_op jit(solution)/shard_map/ppermute | solution.py:21
  21.1 0.7 fusion.25
  21.8 1.1 iota_compare_fusion
  23.0 1.4 %fusion.12 = f32[2,256,256]{2,1,0:T(8,128)S(1)} fusion(f32[2,256,256]{2,1,0:T(8,128)S(1)} %bitcast.87, pred[8,256,256]{2,1,0:T(32,128)(4,1)} %iota_compare_fusion, s32[]{:T(128)S(6)} %select_n.26), kind=kOutput, calls=%fused_computation.42 | convolution fusion | flops 402653184 | bytes 1179652 | tf_op jit(solution)/shard_map/bik,bkj->bij/dot_general | solution.py:33
  24.4 1.3 %fusion.10 = f32[2,256,256]{2,1,0:T(8,128)S(1)} fusion(f32[2,256,256]{2,1,0:T(8,128)S(1)} %fusion.12, pred[8,256,256]{2,1,0:T(32,128)(4,1)} %iota_compare_fusion, s32[]{:T(128)S(6)} %select_n.26), kind=kOutput, calls=%fused_computation.40 | convolution fusion | flops 402653184 | bytes 1179652 | tf_op jit(solution)/shard_map/bik,bjk->bij/dot_general | solution.py:33
  25.7 0.6 convolution_subtract_fusion.5
  26.3 0.9 fusion.37
  27.2 0.9 slice.151
  28.1 0.7 slice.152
  28.8 0.5 convolution_subtract_fusion.4
  29.3 10.5 %copy.75 = f32[2,192,192]{0,2,1:T(8,128)} copy(f32[2,192,192]{2,1,0:T(8,128)} %slice.151) | data formatting | bytes 589824 | tf_op jit(solution)/shard_map/slice | solution.py:51
  39.8 5.3 %gather_fusion = f32[192,2]{1,0:T(8,128)} fusion(f32[2,192,192]{0,2,1:T(8,128)} %copy.75, s32[192]{0:T(256)S(1)} %bitcast.85), kind=kCustom, calls=%fused_computation | custom fusion | bytes 4608 | tf_op jit(solution)/shard_map/jit(diagonal)/gather | solution.py:62
  45.1 1.0 copy.76
  46.1 1.5 %convolution_add_fusion = f32[2,192,192]{2,1,0:T(8,128)S(1)} fusion(f32[2,192,192]{2,1,0:T(8,128)S(1)} %convolution_subtract_fusion.4, f32[2,64,192]{2,1,0:T(8,128)} %fusion.37, f32[8,64,192]{2,1,0:T(8,128)S(1)} %copy-done, s32[]{:T(128)S(6)} %select_n.26), kind=kOutput, calls=%fused_computation.12 | convolution fusion | flops 56696832 | bytes 917508 | tf_op jit(solution)/shard_map/bji,bjk->bik/dot_general | solution.py:33
  47.6 1.5 %fusion.14 = f32[2,192,192]{2,1,0:T(8,128)S(1)} fusion(f32[2,192,192]{2,1,0:T(8,128)S(1)} %convolution_add_fusion, f32[2,192]{1,0:T(2,128)S(1)} %copy.76, f32[192,192]{1,0:T(8,128)} %fusion.25), kind=kOutput, calls=%fused_computation.44 | convolution fusion | flops 169943040 | bytes 738816 | tf_op jit(solution)/shard_map/bij,bjk->bik/dot_general | solution.py:33
  49.1 0.6 convolution_subtract_fusion.8
  49.6 0.5 fusion.53
  50.2 0.5 convolution_subtract_fusion.7
  50.7 0.5 fusion.54
  51.2 0.5 convolution_subtract_fusion.6
  51.8 2.1 %fusion.29 = f32[2,64,192]{2,1,0:T(8,128)} fusion(f32[2,192,192]{2,1,0:T(8,128)S(1)} %convolution_subtract_fusion.6, f32[2,64,192]{2,1,0:T(8,128)} %fusion.37, f32[2,256,256]{2,1,0:T(8,128)S(1)} %fusion.10), kind=kOutput, calls=%fused_computation.62 | convolution fusion | flops 56647680 | bytes 720896 | tf_op jit(solution)/shard_map/bij,bjk->bik/dot_general | solution.py:33
  53.9 0.0 all-gather.2.cloned.1.call-update
  53.9 1.7 %copy.96 = f32[2,192,64]{1,2,0:T(8,128)} copy(f32[2,192,64]{2,1,0:T(8,128)} %slice.152) | data formatting | bytes 196608
  55.7 1.2 convolution_subtract_fusion.13
  56.9 1.2 convolution_subtract_fusion.14
  58.1 6.9 %all_gather.20 = f32[8,64,64]{2,1,0:T(8,128)S(1)} all-gather(f32[2,64,64]{2,1,0:T(8,128)S(1)} %convolution_subtract_fusion.14), channel_id=1, replica_groups=mesh['box'=8,'nbr'=4] {'nbr'}, dimensions={0}, use_global_device_ids=true | all-gather | bytes 163840 | tf_op jit(solution)/shard_map/all_gather | solution.py:105
  65.0 10.5 %all_gather.25 = f32[8,64,192]{2,1,0:T(8,128)S(1)} all-gather(f32[2,64,192]{2,1,0:T(8,128)} %fusion.29), channel_id=1, replica_groups=mesh['box'=8,'nbr'=4] {'nbr'}, dimensions={0}, use_global_device_ids=true | all-gather | bytes 491520 | tf_op jit(solution)/shard_map/all_gather | solution.py:103
  75.5 0.5 fusion.57
  76.1 7.5 %all_gather.26 = f32[8,192,64]{1,2,0:T(8,128)S(1)} all-gather(f32[2,192,64]{1,2,0:T(8,128)S(1)} %fusion.57), channel_id=1, replica_groups=mesh['box'=8,'nbr'=4] {'nbr'}, dimensions={0}, use_global_device_ids=true | all-gather | bytes 491520 | tf_op jit(solution)/shard_map/all_gather | solution.py:104
  83.5 2.0 %pad_maximum_fusion = f32[16,2,2,64,256]{4,3,2,1,0:T(8,128)S(1)} fusion(f32[4,2,2,64,256]{4,3,2,1,0:T(8,128)} %collective-permute-done.1, f32[8,2,2,64,256]{4,3,2,1,0:T(8,128)S(1)} %broadcast_multiply_fusion, f32[4,2,2,64,256]{4,3,2,1,0:T(8,128)} %collective-permute-done), kind=kLoop, calls=%fused_computation.1 | loop fusion | flops 2097152 | bytes 8388608 | tf_op jit(solution)/shard_map/concatenate | solution.py:22
  85.6 0.4 fusion.50
  86.0 1.6 %fusion.2 = f32[8,2,64,256]{3,2,0,1:T(8,128)S(1)} fusion(s32[8,256]{1,0:T(8,128)S(1)} %copy-done.5, f32[16,1,2,64,256]{4,3,2,1,0:T(8,128)S(1)} %get-tuple-element.42, s32[]{:T(128)S(6)} %select_n.30), kind=kOutput, calls=%fused_computation.5 | convolution fusion | flops 805830656 | bytes 2105348 | tf_op jit(solution)/shard_map/bpik,bjk->bpij/dot_general | solution.py:33
  87.6 0.1 slice_bitcast_fusion
  87.7 0.6 convolution_subtract_fusion
  88.3 0.6 convolution_subtract_fusion.1
  88.8 1.6 %fusion = f32[8,2,64,256]{3,2,1,0:T(8,128)S(1)} fusion(f32[16,1,2,64,256]{4,3,2,1,0:T(8,128)S(1)} %get-tuple-element.43, s32[]{:T(128)S(6)} %select_n.28, s32[8,256]{1,0:T(8,128)S(1)} %copy-done.5), kind=kOutput, calls=%fused_computation.3 | convolution fusion | flops 805830656 | bytes 2105348 | tf_op jit(solution)/shard_map/bpik,bjk->bpij/dot_general | solution.py:33
  90.4 0.1 slice_bitcast_fusion.2
  90.5 0.6 convolution_subtract_fusion.2
  91.1 0.6 convolution_subtract_fusion.3
  91.7 0.7 convolution_subtract_fusion.10
  92.4 0.7 convolution_subtract_fusion.12
  93.0 0.7 convolution_subtract_fusion.9
  93.7 0.7 convolution_subtract_fusion.11
  94.4 0.1 maximum_bitcast_fusion
  94.5 1.1 pad_maximum_fusion.1
  95.5 2.3 %copy.87 = f32[8,2,64,128]{3,2,1,0:T(8,128)} copy(f32[8,2,64,128]{2,3,0,1:T(8,128)} %pad_maximum_fusion.1) | data formatting | bytes 1048576
  97.9 2.6 %fusion.55 = f32[8,64,192]{2,1,0:T(8,128)S(1)} fusion(f32[8,64,192]{2,1,0:T(8,128)S(1)} %convolution_subtract_fusion.3, f32[8,192,192]{2,1,0:T(8,128)} %all-gather.2.cloned.1.call-done), kind=kOutput, calls=%fused_computation.90 | convolution fusion | flops 226492416 | bytes 1966080 | tf_op jit(solution)/shard_map/bij,bjk->bik/dot_general | solution.py:33
  100.6 0.6 convolution_dynamic-update-slice_fusion
  101.2 1.1 fusion.56
  102.4 0.6 fusion.4
  103.1 1.8 %collective-permute-start.2 = (f32[4,64,64]{2,1,0:T(8,128)S(1)}, f32[4,64,64]{2,1,0:T(8,128)S(1)}, u32[]{:S(2)}, u32[]{:S(2)}) collective-permute-start(f32[4,64,64]{2,1,0:T(8,128)S(1)} %get-tuple-element.51), channel_id=1, source_target_pairs={{4,0},{8,4},{12,8},{16,12},{20,16},{24,20},{28,24},{0,28},{5,1},{9... | collective-permute-start | bytes 196616 | tf_op jit(solution)/shard_map/ppermute | solution.py:29
  104.8 0.3 collective-permute-start.3
  105.2 0.8 constant_dynamic-slice_fusion
  105.9 2.9 %collective-permute-done.2 = f32[4,64,64]{2,1,0:T(8,128)S(1)} collective-permute-done((f32[4,64,64]{2,1,0:T(8,128)S(1)}, f32[4,64,64]{2,1,0:T(8,128)S(1)}, u32[]{:S(2)}, u32[]{:S(2)}) %collective-permute-start.2) | collective-permute-done | bytes 65568 | tf_op jit(solution)/shard_map/ppermute | solution.py:29
  108.9 4.1 %collective-permute-done.3 = f32[4,64,64]{2,1,0:T(8,128)S(1)} collective-permute-done((f32[4,64,64]{2,1,0:T(8,128)S(1)}, f32[4,64,64]{2,1,0:T(8,128)S(1)}, u32[]{:S(2)}, u32[]{:S(2)}) %collective-permute-start.3) | collective-permute-done | bytes 65568 | tf_op jit(solution)/shard_map/ppermute | solution.py:29
  113.0 9.9 %all_gather.24 = f32[4,8,64,64]{3,2,1,0:T(8,128)S(1)} all-gather(f32[1,8,64,64]{3,2,1,0:T(8,128)S(1)} %fusion.27), channel_id=1, replica_groups=mesh['box'=8,'nbr'=4] {'nbr'}, dimensions={0}, use_global_device_ids=true | all-gather | bytes 655360 | tf_op jit(solution)/shard_map/all_gather | solution.py:130
  122.9 0.1 reduce_sum.9
  123.0 0.7 sub.80
  (25 shorter events, 0.2 us)
Async XLA Ops:
  7.2 18.5 %copy-start = (f32[8,64,192]{2,1,0:T(8,128)S(1)}, f32[8,64,192]{2,1,0:T(8,128)}, u32[]{:S(2)}) copy-start(f32[8,64,192]{2,1,0:T(8,128)} %param.11) | copy-start | bytes 1179652
  7.2 15.8 %all-to-all-start = ((f32[8,64,256]{2,1,0:T(8,128)}), f32[8,64,256]{2,1,0:T(8,128)S(1)}, u32[]{:S(2)}, u32[]{:S(2)}) async-start(f32[8,64,256]{2,1,0:T(8,128)} %param.9), calls=%async_computation | async-start | bytes 1048576 | tf_op jit(solution)/shard_map/all_to_all | solution.py:97
  11.6 86.3 %all-gather.2.cloned.1.call-start = ((), (), s32[]{:S(2)}) async-start(), calls=%async_computation.1 | async-start | bytes 1966080 | tf_op jit(solution)/shard_map/all_gather | solution.py:102
  14.2 7.6 %copy-start.5 = (s32[8,256]{1,0:T(8,128)S(1)}, s32[8,256]{1,0:T(8,128)}, u32[]{:S(2)}) copy-start(s32[8,256]{1,0:T(8,128)} %param.10) | copy-start | bytes 24580
  15.8 67.7 %collective-permute-start = (f32[4,2,2,64,256]{4,3,2,1,0:T(8,128)}, f32[4,2,2,64,256]{4,3,2,1,0:T(8,128)}, u32[]{:S(2)}, u32[]{:S(2)}) collective-permute-start(f32[4,2,2,64,256]{4,3,2,1,0:T(8,128)} %get-tuple-element.44), channel_id=1, source_target_pairs={{0,4},{4,8},{8,12},{12,16},{16,20},{20,24},{24,28},{28,0},{1,5},{5... | collective-permute-start | bytes 3145736 | tf_op jit(solution)/shard_map/ppermute | solution.py:18
  18.1 65.5 %collective-permute-start.1 = (f32[4,2,2,64,256]{4,3,2,1,0:T(8,128)}, f32[4,2,2,64,256]{4,3,2,1,0:T(8,128)}, u32[]{:S(2)}, u32[]{:S(2)}) collective-permute-start(f32[4,2,2,64,256]{4,3,2,1,0:T(8,128)} %get-tuple-element.45), channel_id=1, source_target_pairs={{4,0},{8,4},{12,8},{16,12},{20,16},{24,20},{28,24},{0,28},{5,1},{9... | collective-permute-start | bytes 3145736 | tf_op jit(solution)/shard_map/ppermute | solution.py:21
  46.1 3.0 %copy-start.4 = (f32[192,192]{1,0:T(8,128)S(1)}, f32[192,192]{1,0:T(8,128)}, u32[]{:S(2)}) copy-start(f32[192,192]{1,0:T(8,128)} %fusion.25) | copy-start | bytes 442372
  51.8 2.1 %copy-start.2 = (f32[2,192,192]{2,1,0:T(8,128)}, f32[2,192,192]{2,1,0:T(8,128)S(1)}, u32[]{:S(2)}) copy-start(f32[2,192,192]{2,1,0:T(8,128)S(1)} %convolution_subtract_fusion.6) | copy-start | bytes 884740
  53.9 21.6 %copy-start.3 = (f32[2,192,192]{2,1,0:T(8,128)S(1)}, f32[2,192,192]{2,1,0:T(8,128)}, u32[]{:S(2)}) copy-start(f32[2,192,192]{2,1,0:T(8,128)} %copy-done.2) | copy-start | bytes 884740
  97.9 3.3 %copy-start.1 = (f32[8,192,192]{2,1,0:T(8,128)S(1)}, f32[8,192,192]{2,1,0:T(8,128)}, u32[]{:S(2)}) copy-start(f32[8,192,192]{2,1,0:T(8,128)} %all-gather.2.cloned.1.call-done) | copy-start | bytes 3538948
  103.1 5.8 %collective-permute-start.2 = (f32[4,64,64]{2,1,0:T(8,128)S(1)}, f32[4,64,64]{2,1,0:T(8,128)S(1)}, u32[]{:S(2)}, u32[]{:S(2)}) collective-permute-start(f32[4,64,64]{2,1,0:T(8,128)S(1)} %get-tuple-element.51), channel_id=1, source_target_pairs={{4,0},{8,4},{12,8},{16,12},{20,16},{24,20},{28,24},{0,28},{5,1},{9... | collective-permute-start | bytes 196616 | tf_op jit(solution)/shard_map/ppermute | solution.py:29
  104.8 8.2 %collective-permute-start.3 = (f32[4,64,64]{2,1,0:T(8,128)S(1)}, f32[4,64,64]{2,1,0:T(8,128)S(1)}, u32[]{:S(2)}, u32[]{:S(2)}) collective-permute-start(f32[4,64,64]{2,1,0:T(8,128)S(1)} %get-tuple-element.50), channel_id=1, source_target_pairs={{28,0},{0,4},{4,8},{8,12},{12,16},{16,20},{20,24},{24,28},{29,1},{... | collective-permute-start | bytes 196616 | tf_op jit(solution)/shard_map/ppermute | solution.py:29
Sparse Core Ops, SparseCore 0:
  54.0 21.4 all-gather.1
